TPU v7x, 32 devices: a whole 2x2x4 slice. The times are simulated.
32 devices in a mesh: aa: 4 (over x, core), ba: 4 (over z), col: 2 (over y).
Axes of the slice: x: 2, y: 2, z: 4, core: 2. Of those that a mesh axis runs over, the one named last changes fastest.
Arguments:
- tokens: bfloat16 [64, 32, 64, 1024], P('aa', 'ba', 'col'), may hold values from -6 to 6
- norm_gain: float32 [1024], replicated, may hold values from 0.1 to 1.9
- in_weight: bfloat16 [1024, 3072], replicated, may hold values from -0.1875 to 0.1875
- skip_gain: float32 [1024], replicated, may hold values from 0.5 to 1.5
- spectrum_filter: bfloat16 [2, 64, 32, 64, 1024], P(None, ('ba', 'col'), None, None, 'aa'), may hold values from -4 to 4
- out_weight: bfloat16 [1024, 1024], replicated, may hold values from -0.1875 to 0.1875
Outputs:
- layer_out: bfloat16 [64, 32, 64, 1024], P('aa', 'ba', 'col')
All inputs are finite; a program needn't handle non-finite values.
Results may differ from a plain program's by a relative error of at most 0.014.
Values may be sent and summed in bfloat16 or wider, within the bound.
A program may use at most 256 MiB of HBM per device.

v0:
```python
import math
import jax
import jax.numpy as jnp
from jax import lax
from jax.sharding import PartitionSpec as P

LA = 64
LB = 32
LC = 64
D = 1024
EPSILON = 1e-06


def dft_tables(length):
    counter = jnp.arange(length, dtype=jnp.int32)
    product = counter[:, None] * counter[None, :] % length
    angle = 2.0 * math.pi / length * product.astype(jnp.float32)
    factor = 1.0 / math.sqrt(length)
    return (
        (jnp.cos(angle) * factor).astype(jnp.bfloat16),
        (jnp.sin(angle) * factor).astype(jnp.bfloat16),
    )


def phase_pair(integer_phase, modulus):
    angle = 2.0 * math.pi / modulus * (integer_phase % modulus).astype(jnp.float32)
    return (jnp.cos(angle), jnp.sin(angle))


def contract(form, table, operand):
    return jnp.einsum(form, table, operand, preferred_element_type=jnp.float32)


def local(tokens, norm_gain, in_weight, skip_gain, spectrum_filter, out_weight):
    count_aa = lax.axis_size("aa")
    count_ba = lax.axis_size("ba")
    count_col = lax.axis_size("col")
    rows_i = LA // count_aa
    rows_j = LB // count_ba
    rows_k = LC // count_col
    blocks = count_ba * count_col
    freq_local = LA // blocks
    channels = D // count_aa
    points = LA * LB * LC
    flat = tokens.reshape(-1, D).astype(jnp.float32)
    meansq = jnp.mean(flat * flat, axis=-1, keepdims=True)
    normed = (flat * lax.rsqrt(meansq + EPSILON) * norm_gain).astype(jnp.bfloat16)
    projected = jnp.dot(normed, in_weight, preferred_element_type=jnp.float32)
    mixed = (projected[:, :D] * projected[:, 2 * D :]).astype(jnp.bfloat16)
    gate = projected[:, D : 2 * D].astype(jnp.bfloat16)
    local_block = mixed.reshape(rows_i, rows_j, rows_k, D)
    by_rows = lax.all_to_all(local_block, "aa", split_axis=3, concat_axis=0, tiled=True)
    cos_a, sin_a = dft_tables(LA)
    real_part = contract("fi,ijkx->fjkx", cos_a, by_rows)
    imag_part = -contract("fi,ijkx->fjkx", sin_a, by_rows)
    j_global = lax.axis_index("ba") * rows_j + jnp.arange(rows_j, dtype=jnp.int32)
    k_global = lax.axis_index("col") * rows_k + jnp.arange(rows_k, dtype=jnp.int32)
    freq_all = jnp.arange(LA, dtype=jnp.int32)
    cos_phi, sin_phi = phase_pair(
        (LC * j_global[None, :, None] + k_global[None, None, :]) * freq_all[:, None, None], points
    )
    cos_phi = cos_phi[..., None]
    sin_phi = sin_phi[..., None]
    first = jnp.stack(
        [real_part * cos_phi + imag_part * sin_phi, imag_part * cos_phi - real_part * sin_phi]
    ).astype(jnp.bfloat16)
    shaped = first.reshape(2, blocks, 1, freq_local, rows_j, rows_k, channels)
    moved = lax.all_to_all(shaped, ("ba", "col"), split_axis=1, concat_axis=2, tiled=True)
    moved = moved.reshape(2, count_ba, count_col, freq_local, rows_j, rows_k, channels)
    cos_b, sin_b = dft_tables(LB)
    cos_b = cos_b.reshape(LB, count_ba, rows_j)
    sin_b = sin_b.reshape(LB, count_ba, rows_j)
    moved_real = moved[0]
    moved_imag = moved[1]
    form_two = "gbj,bcfjkx->fgckx"
    real_part = contract(form_two, cos_b, moved_real) + contract(form_two, sin_b, moved_imag)
    imag_part = contract(form_two, cos_b, moved_imag) - contract(form_two, sin_b, moved_real)
    index_g = jnp.arange(LB, dtype=jnp.int32)
    index_k = jnp.arange(LC, dtype=jnp.int32)
    cos_psi, sin_psi = phase_pair(index_g[:, None] * index_k[None, :], LB * LC)
    cos_psi = cos_psi.reshape(1, LB, count_col, rows_k, 1)
    sin_psi = sin_psi.reshape(1, LB, count_col, rows_k, 1)
    second_real = (real_part * cos_psi + imag_part * sin_psi).astype(jnp.bfloat16)
    second_imag = (imag_part * cos_psi - real_part * sin_psi).astype(jnp.bfloat16)
    cos_c, sin_c = dft_tables(LC)
    cos_c = cos_c.reshape(LC, count_col, rows_k)
    sin_c = sin_c.reshape(LC, count_col, rows_k)
    form_three = "hck,fgckx->fghx"
    spec_real = contract(form_three, cos_c, second_real) + contract(form_three, sin_c, second_imag)
    spec_imag = contract(form_three, cos_c, second_imag) - contract(form_three, sin_c, second_real)
    filt_real = spectrum_filter[0].astype(jnp.float32)
    filt_imag = spectrum_filter[1].astype(jnp.float32)
    filtered_real = (filt_real * spec_real - filt_imag * spec_imag).astype(jnp.bfloat16)
    filtered_imag = (filt_real * spec_imag + filt_imag * spec_real).astype(jnp.bfloat16)
    form_back_three = "hck,fghx->fgckx"
    real_part = contract(form_back_three, cos_c, filtered_real) - contract(
        form_back_three, sin_c, filtered_imag
    )
    imag_part = contract(form_back_three, cos_c, filtered_imag) + contract(
        form_back_three, sin_c, filtered_real
    )
    third_real = (real_part * cos_psi - imag_part * sin_psi).astype(jnp.bfloat16)
    third_imag = (imag_part * cos_psi + real_part * sin_psi).astype(jnp.bfloat16)
    form_back_two = "gbj,fgckx->bcfjkx"
    real_part = contract(form_back_two, cos_b, third_real) - contract(
        form_back_two, sin_b, third_imag
    )
    imag_part = contract(form_back_two, cos_b, third_imag) + contract(
        form_back_two, sin_b, third_real
    )
    slot = lax.axis_index("ba") * count_col + lax.axis_index("col")
    freq_global = slot * freq_local + jnp.arange(freq_local, dtype=jnp.int32)
    j_all = jnp.arange(LB, dtype=jnp.int32).reshape(count_ba, rows_j)
    k_all = jnp.arange(LC, dtype=jnp.int32).reshape(count_col, rows_k)
    integer_phase = (
        LC * j_all[:, None, None, :, None] + k_all[None, :, None, None, :]
    ) * freq_global[None, None, :, None, None]
    cos_back, sin_back = phase_pair(integer_phase, points)
    cos_back = cos_back[..., None]
    sin_back = sin_back[..., None]
    back_second = jnp.stack(
        [real_part * cos_back - imag_part * sin_back, imag_part * cos_back + real_part * sin_back]
    ).astype(jnp.bfloat16)
    shaped = back_second.reshape(2, 1, blocks, freq_local, rows_j, rows_k, channels)
    returned = lax.all_to_all(shaped, ("ba", "col"), split_axis=2, concat_axis=1, tiled=True)
    returned = returned.reshape(2, LA, rows_j, rows_k, channels)
    conv_part = (
        contract("fi,fjkx->ijkx", cos_a, returned[0])
        - contract("fi,fjkx->ijkx", sin_a, returned[1])
    ).astype(jnp.bfloat16)
    conv_tokens = lax.all_to_all(conv_part, "aa", split_axis=0, concat_axis=3, tiled=True)
    conv_flat = conv_tokens.reshape(-1, D).astype(jnp.float32)
    gated = (gate.astype(jnp.float32) * (conv_flat + skip_gain * mixed.astype(jnp.float32))).astype(
        jnp.bfloat16
    )
    layer_out = jnp.dot(gated, out_weight, preferred_element_type=jnp.float32).astype(jnp.bfloat16)
    return layer_out.reshape(rows_i, rows_j, rows_k, D)


def solution(mesh):
    in_specs = (
        P("aa", "ba", "col", None),
        P(),
        P(),
        P(),
        P(None, ("ba", "col"), None, None, "aa"),
        P(),
    )
    out_specs = P("aa", "ba", "col", None)
    return jax.shard_map(local, mesh=mesh, in_specs=in_specs, out_specs=out_specs, check_vma=False)
```

profile of v0, /device:TPU:0, one launch (start us, length us, event | category | flops | bytes accessed | tf_op | source)
XLA Modules:
  0.0 1626.5 jit_solution(17985871560991421885)
XLA Ops:
  0.0 5.2 multiply_reduce_fusion
  5.3 0.1 rsqrt.12
  5.4 0.0 copy-done.7
  5.4 0.0 copy-start.8
  5.4 5.4 fusion.14
  10.8 31.4 %fusion.236 = f32[4096,3072]{1,0:T(8,128)} fusion(bf16[4096,1024]{1,0:T(8,128)(2,1)S(1)} %fusion.14, bf16[1024,3072]{1,0:T(8,128)(2,1)S(1)} %copy-done.8), kind=kOutput, calls=%fused_computation.280 | convolution fusion | flops 25769803776 | bytes 65011712 | tf_op jit(solution)/shard_map/dot_general | solution.py:48
  42.2 15.1 fusion.4
  57.4 44.2 %copy.74 = bf16[16,8,32,1024]{2,1,0,3:T(8,128)(2,1)} copy(bf16[16,8,32,1024]{3,2,1,0:T(8,128)(2,1)} %bitcast.244) | data formatting | bytes 16777216 | tf_op jit(solution)/shard_map/reshape | solution.py:51
  101.6 50.4 %reshape.452 = bf16[4,2,524288]{2,1,0:T(2,128)(2,1)} reshape(bf16[1024,16,8,32]{3,2,1,0:T(8,128)(2,1)} %bitcast.236) | data formatting | bytes 16777216
  152.0 6.1 all-to-all-start
  158.1 0.1 broadcast_add_fusion.1
  158.2 1.3 fusion.61
  159.5 92.4 %all-to-all-done = bf16[4,2,524288]{2,1,0:T(2,128)(2,1)} async-done(((bf16[4,2,524288]{2,1,0:T(2,128)(2,1)}), bf16[4,2,524288]{2,1,0:T(2,128)(2,1)}, u32[]{:S(2)}, u32[]{:S(2)}) %all-to-all-start) | async-done | bytes 8388640 | tf_op jit(solution)/shard_map/all_to_all | solution.py:52
  251.9 37.0 %reshape.453 = bf16[1024,16,8,32]{3,2,1,0:T(8,128)(2,1)} reshape(bf16[4,2,524288]{2,1,0:T(2,128)(2,1)} %all-to-all-done) | data formatting | bytes 16777216
  288.9 45.4 %copy.75 = bf16[16,8,32,4,256]{4,0,3,2,1:T(8,128)(2,1)} copy(bf16[16,8,32,4,256]{2,1,0,4,3:T(8,128)(2,1)} %bitcast.235) | data formatting | bytes 16777216 | tf_op jit(solution)/shard_map/all_to_all | solution.py:52
  334.3 6.0 fusion.107
  340.3 11.3 fusion.15
  351.6 11.4 copy.78
  363.0 11.4 copy.79
  374.4 13.8 pad_maximum_fusion
  388.2 6.6 all-to-all-start.1
  394.8 0.2 fusion.103
  395.0 0.1 copy.90
  395.1 0.1 copy.91
  395.2 0.1 broadcast_add_fusion
  395.3 1.1 fusion.56
  396.4 1.4 copy.94
  397.7 1.4 copy.97
  399.1 358.3 %all-to-all-done.1 = bf16[2,8,1,8,8,32,256]{6,5,4,3,2,0,1:T(8,128)(2,1)} async-done(((bf16[2,8,1,8,8,32,256]{6,5,4,3,2,0,1:T(8,128)(2,1)}), bf16[2,8,1,8,8,32,256]{6,5,4,3,2,0,1:T(8,128)(2,1)}, u32[]{:S(2)}, u32[]{:S(2)}) %all-to-all-start.1) | async-done | bytes 16777248 | tf_op jit(solution)/shard_map/all_to_all | solution.py:68
  757.4 10.3 fusion.227
  767.8 0.0 copy-start.4
  767.8 17.5 %fusion.45 = f32[2,8,32,256,32,1]{3,4,5,2,1,0:T(8,128)} fusion(bf16[4,2,8,8,32,256]{5,4,3,2,1,0:T(8,128)(2,1)} %bitcast.241, s32[4,8]{1,0:T(4,128)S(1)} %multiply_add_fusion), kind=kOutput, calls=%fused_computation.77 | convolution fusion | flops 268451840 | bytes 25165952 | tf_op jit(solution)/shard_map/gbj,bcfjkx->fgckx/dot_general | solution.py:31
  785.3 14.3 fusion.47
  799.6 0.0 copy-done.4
  799.6 8.9 fusion.41
  808.5 26.6 %fusion.10 = (bf16[8,32,2,32,256]{4,1,3,0,2:T(8,128)(2,1)}, bf16[8,32,2,32,256]{4,1,3,0,2:T(8,128)(2,1)}) fusion(f32[32,2,32]{0,2,1:T(8,128)S(1)} %get-tuple-element.24, f32[32,2,32]{0,2,1:T(8,128)S(1)} %get-tuple-element.23, f32[2,8,32,256,32,1]{3,4,5,2,1,0:T(8,128)} %fusion.47, f32[2,8,32,256,32,1]{3,4,5,2,1,0:T(8,128)} %fusion.45, ...), kind=kOutput, calls=%fused_computation.26 | convolution fusion | flops 310394880 | bytes 75513984 | tf_op jit(solution)/shard_map/gbj,bcfjkx->fgckx/dot_general | solution.py:31
  835.2 16.0 fusion.35
  851.2 0.0 copy-done.1
  851.2 12.4 fusion.39
  863.5 21.3 %bitcast_subtract_fusion = f32[8,32,256,64]{2,3,1,0:T(8,128)} fusion(f32[8,32,256,64,1]{2,3,4,1,0:T(8,128)} %fusion.35, bf16[8,32,2,32,256]{4,1,3,0,2:T(8,128)(2,1)} %get-tuple-element.5, s32[2,32]{1,0:T(2,128)S(1)} %multiply_add_fusion.1), kind=kOutput, calls=%fused_computation.21 | convolution fusion | flops 541130752 | bytes 41943296 | tf_op jit(solution)/shard_map/hck,fgckx->fghx/dot_general | solution.py:31
  884.8 24.5 %fusion.20 = (bf16[8,32,64,256,1]{3,2,4,1,0:T(8,128)(2,1)}, bf16[8,32,64,256,1]{3,2,4,1,0:T(8,128)(2,1)S(1)}) fusion(f32[8,32,256,64]{2,3,1,0:T(8,128)} %bitcast_subtract_fusion, bf16[2,8,32,64,256]{4,3,2,1,0:T(8,128)(2,1)} %param.10, s32[2,32]{1,0:T(2,128)S(1)} %multiply_add_fusion.1, bf16[8,32,2,32,256]{4,1,3,0,2:T(8,128)(2,1)} %get-tuple-element.6, ...), kind=kOutput, calls=%fused_computation.52 | convolution fusion | flops 583073792 | bytes 75497728 | tf_op jit(solution)/shard_map/hck,fgckx->fghx/dot_general | solution.py:31
  909.3 11.7 fusion.96
  921.0 8.2 fusion.98
  929.2 14.1 convolution_add_fusion.1
  943.3 19.4 %fusion.17 = (bf16[8,32,2,32,256,1]{4,3,2,1,0,5:T(8,128)(2,1)S(1)}, bf16[8,32,2,32,256,1]{4,3,2,1,0,5:T(8,128)(2,1)}) fusion(f32[8,32,256,2,32]{2,4,3,1,0:T(8,128)} %convolution_add_fusion.1, f32[32,2,32]{2,1,0:T(2,128)S(1)} %copy.91, f32[32,2,32]{2,1,0:T(2,128)S(1)} %copy.90, f32[8,32,256,2,32]{2,4,3,1,0:T(8,128)} %fusion.98, ...), kind=kOutput, calls=%fused_computation.49 | convolution fusion | flops 574685184 | bytes 58736896 | tf_op jit(solution)/shard_map/hck,fghx->fgckx/dot_general | solution.py:31
  962.6 11.0 fusion.33
  973.7 14.3 fusion.29
  988.0 20.0 %convolution_subtract_fusion = f32[8,2,32,256,4,8]{3,5,4,2,1,0:T(8,128)} fusion(f32[8,2,32,256,4,8]{3,5,4,2,1,0:T(8,128)} %fusion.33, bf16[8,32,2,32,256,1]{4,3,2,1,0,5:T(8,128)(2,1)} %get-tuple-element.14, s32[4,8]{1,0:T(4,128)S(1)} %multiply_add_fusion), kind=kOutput, calls=%fused_computation.44 | convolution fusion | flops 272646144 | bytes 41943168 | tf_op jit(solution)/shard_map/gbj,fgckx->bcfjkx/dot_general | solution.py:31
  1008.0 23.1 %fusion.6 = (bf16[4,2,8,8,32,256]{5,3,0,4,1,2:T(8,128)(2,1)}, bf16[4,2,8,8,32,256]{5,3,0,4,1,2:T(8,128)(2,1)}) fusion(f32[8,2,32,256,4,8]{3,5,4,2,1,0:T(8,128)} %convolution_subtract_fusion, f32[4,2,8,8,32]{3,0,4,1,2:T(4,128)S(1)} %copy-done.6, f32[4,2,8,8,32]{3,0,4,1,2:T(4,128)S(1)} %copy-done.5, f32[8,2,32,256,4,8]{3,5,4,2,1,0:T(8,128)} %fusion.29, ...), kind=kOutput, calls=%fused_computation.16 | convolution fusion | flops 306200576 | bytes 58851456 | tf_op jit(solution)/shard_map/gbj,fgckx->bcfjkx/dot_general | solution.py:31
  1031.1 15.7 copy.98
  1046.9 15.9 copy.99
  1062.8 8.0 pad_maximum_fusion.1
  1070.8 6.8 copy.100
  1077.5 367.5 %all_to_all.45 = bf16[2,1,8,8,8,32,256]{6,5,4,3,1,0,2:T(8,128)(2,1)S(1)} all-to-all(bf16[2,1,8,8,8,32,256]{6,5,4,3,1,0,2:T(8,128)(2,1)} %copy.100), channel_id=1, replica_groups=mesh['aa'=4,'ba'=4,'col'=2] {'ba','col'}, dimensions={2} | all-to-all | bytes 33554432 | tf_op jit(solution)/shard_map/all_to_all | solution.py:125
  1445.1 5.0 fusion.226
  1450.0 12.5 fusion.23
  1462.5 21.2 %subtract_convert_fusion = bf16[64,8,32,256]{3,0,2,1:T(8,128)(2,1)} fusion(f32[64,8,32,256]{3,0,2,1:T(8,128)} %fusion.23, bf16[1,1,8,8,8,32,256]{6,5,4,3,1,0,2:T(8,128)(2,1)} %get-tuple-element.15), kind=kOutput, calls=%fused_computation.37 | convolution fusion | flops 545325056 | bytes 33554432 | tf_op jit(solution)/shard_map/fi,fjkx->ijkx/dot_general | solution.py:31
  1483.7 11.4 copy.103
  1495.1 97.2 %all_to_all.46 = bf16[64,8,32,256]{3,2,1,0:T(8,128)(2,1)S(1)} all-to-all(bf16[64,8,32,256]{3,2,1,0:T(8,128)(2,1)} %copy.103), channel_id=1, replica_groups=mesh['aa'=4,'ba'=4,'col'=2] {'aa'}, dimensions={0} | all-to-all | bytes 16777216 | tf_op jit(solution)/shard_map/all_to_all | solution.py:131
  1592.3 6.9 copy.104
  1599.1 0.0 slice-start.1
  1599.1 0.0 copy-start.9
  1599.2 8.2 copy.141
  1607.4 18.7 %fusion.28 = bf16[4096,1024]{1,0:T(8,128)(2,1)} fusion(bf16[1024,1024]{1,0:T(8,128)(2,1)S(1)} %copy-done, f32[4096,1024]{1,0:T(8,128)} %bitcast.250, bf16[4096,1024]{1,0:T(8,128)(2,1)S(1)} %bitcast.246, f32[4096,3072]{1,0:T(8,128)} %fusion.236, f32[1024]{0:T(1024)S(1)} %copy-done.9), kind=kOutput, calls=%fused_computation.60 | convolution fusion | flops 8619294720 | bytes 44044288 | tf_op jit(solution)/shard_map/dot_general | solution.py:136
  (25 shorter events, 0.1 us)
Async XLA Ops:
  0.0 1607.3 %copy-start = (bf16[1024,1024]{1,0:T(8,128)(2,1)S(1)}, bf16[1024,1024]{1,0:T(8,128)(2,1)}, u32[]{:S(2)}) copy-start(bf16[1024,1024]{1,0:T(8,128)(2,1)} %param.11) | copy-start | bytes 6291460
  0.0 5.4 copy-start.7
  5.4 5.4 copy-start.8
  152.0 99.9 %all-to-all-start = ((bf16[4,2,524288]{2,1,0:T(2,128)(2,1)}), bf16[4,2,524288]{2,1,0:T(2,128)(2,1)}, u32[]{:S(2)}, u32[]{:S(2)}) async-start(bf16[4,2,524288]{2,1,0:T(2,128)(2,1)} %reshape.452), calls=%async_computation | async-start | bytes 16777216 | tf_op jit(solution)/shard_map/all_to_all | solution.py:52
  334.3 6.0 copy-start.3
  388.2 369.3 %all-to-all-start.1 = ((bf16[2,8,1,8,8,32,256]{6,5,4,3,2,0,1:T(8,128)(2,1)}), bf16[2,8,1,8,8,32,256]{6,5,4,3,2,0,1:T(8,128)(2,1)}, u32[]{:S(2)}, u32[]{:S(2)}) async-start(bf16[2,8,1,8,8,32,256]{6,5,4,3,2,0,1:T(8,128)(2,1)} %pad_maximum_fusion), calls=%async_computation.1 | async-start | bytes 33554432 | tf_op jit(solution)/shard_map/all_to_all | solution.py:68
  767.8 31.8 %copy-start.4 = (bf16[1,8,1,8,8,32,256]{6,5,4,3,2,0,1:T(8,128)(2,1)}, bf16[1,8,1,8,8,32,256]{6,5,4,3,2,0,1:T(8,128)(2,1)S(1)}, u32[]{:S(2)}) copy-start(bf16[1,8,1,8,8,32,256]{6,5,4,3,2,0,1:T(8,128)(2,1)S(1)} %get-tuple-element.18) | copy-start | bytes 25165828
  835.2 16.0 copy-start.1
  962.6 11.0 copy-start.2
  988.0 20.0 %copy-start.5 = (f32[4,2,8,8,32]{3,0,4,1,2:T(4,128)S(1)}, f32[4,2,8,8,32]{3,0,4,1,2:T(4,128)}, u32[]{:S(2)}) copy-start(f32[4,2,8,8,32]{3,0,4,1,2:T(4,128)} %copy.94) | copy-start | bytes 196612
  988.0 20.0 %copy-start.6 = (f32[4,2,8,8,32]{3,0,4,1,2:T(4,128)S(1)}, f32[4,2,8,8,32]{3,0,4,1,2:T(4,128)}, u32[]{:S(2)}) copy-start(f32[4,2,8,8,32]{3,0,4,1,2:T(4,128)} %copy.97) | copy-start | bytes 196612
  1592.3 15.1 slice-start
  1599.1 8.2 slice-start.1
  1599.1 8.2 copy-start.9
where the time goes:
time: 1630 us
  blocking collectives  465 us (29%)
  waiting for transfers between devices  451 us (28%)
  matrix products  364 us (22%)
  local copies, waits for them, and re-layouts  283 us (17%)
  other arithmetic  50.3 us (3%)
    all_to_all x1, blocking collectives, local(): lax.all_to_all(shaped, ('ba', 'col'), split_axis=2, concat_axis=1, tiled=...  368 us
    all_to_all x1, waiting for transfers between devices, local(): lax.all_to_all(shaped, ('ba', 'col'), split_axis=1, concat_axis=2, tiled=...  358 us
    dot_general x20, matrix products, contract(): return jnp.einsum(form, table, operand, preferred_element_type=jnp.float32)  314 us
    all_to_all x1, blocking collectives, local(): lax.all_to_all(conv_part, 'aa', split_axis=0, concat_axis=3, tiled=True)  97.2 us
    unnamed x27, local copies, waits for them, and re-layouts  95.7 us
    all_to_all x1, waiting for transfers between devices, local(): lax.all_to_all(local_block, 'aa', split_axis=3, concat_axis=0, tiled=True)  92.4 us
    all_to_all x1, local copies, waits for them, and re-layouts, local(): lax.all_to_all(local_block, 'aa', split_axis=3, concat_axis=0, tiled=True)  45.4 us
    reshape x1, local copies, waits for them, and re-layouts, local(): local_block = mixed.reshape(rows_i, rows_j, rows_k, D)  44.2 us
  transfers between devices with their start and end apart: 2, of which 2 were waited for; matrix products, arithmetic and copies ran while one was open for 0% of the time, Pallas kernels for 0%

commit v1 on v0

--- a/solution.py
+++ b/solution.py
@@ -65,7 +65,19 @@
         [real_part * cos_phi + imag_part * sin_phi, imag_part * cos_phi - real_part * sin_phi]
     ).astype(jnp.bfloat16)
     shaped = first.reshape(2, blocks, 1, freq_local, rows_j, rows_k, channels)
-    moved = lax.all_to_all(shaped, ("ba", "col"), split_axis=1, concat_axis=2, tiled=True)
+    ways, here = (lax.axis_size(("ba", "col")), lax.axis_index(("ba", "col")))
+    width = shaped.shape[1] // ways
+    lengths = list(shaped.shape)
+    lengths[1] = width
+    height = lengths[2]
+    lengths[2] = height * ways
+    full = jnp.zeros(lengths, shaped.dtype)
+    for mask in range(ways):
+        part = lax.dynamic_slice_in_dim(shaped, (here ^ mask) * width, width, axis=1)
+        if mask:
+            part = lax.ppermute(part, ("ba", "col"), [(d, d ^ mask) for d in range(ways)])
+        full = lax.dynamic_update_slice_in_dim(full, part, (here ^ mask) * height, axis=2)
+    moved = full
     moved = moved.reshape(2, count_ba, count_col, freq_local, rows_j, rows_k, channels)
     cos_b, sin_b = dft_tables(LB)
     cos_b = cos_b.reshape(LB, count_ba, rows_j)

time: 1630 us -> 1640 us (level)
  waiting for transfers between devices: 451 us -> 340 us
  blocking collectives: 465 us -> 544 us
  local copies, waits for them, and re-layouts: 283 us -> 324 us
    all_to_all x1 -> x0, waiting for transfers between devices: 358 us -> none  [local(): lax.all_to_all(shaped, ('ba', 'col'), split_axis=1, concat_axis=2, tiled=...]
    ppermute x0 -> x7, waiting for transfers between devices: none -> 247 us  [local(): lax.ppermute(part, ('ba', 'col'), [(d, d ^ mask) for d in range(ways)])]
    all_to_all x1, blocking collectives: 368 us -> 447 us  [local(): lax.all_to_all(shaped, ('ba', 'col'), split_axis=2, concat_axis=1, tiled=...]
    dynamic_update_slice x0 -> x7, local copies, waits for them, and re-layouts: none -> 21.9 us  [local(): lax.dynamic_update_slice_in_dim(full, part, (here ^ mask) * height, axis=2)]
    unnamed x27 -> x36, local copies, waits for them, and re-layouts: 95.7 us -> 112 us
  transfers between devices with their start and end apart: 2 -> 8, of which waited for: 2 -> 5; matrix products, arithmetic and copies ran while one was open for 0% -> 2% of each run, Pallas kernels for 0% -> 0%
where the time goes in v1:
time: 1640 us; the launch traced here: 1630 us
  blocking collectives  544 us (33%)
  matrix products  365 us (22%)
  waiting for transfers between devices  340 us (21%)
  local copies, waits for them, and re-layouts  324 us (20%)
  other arithmetic  36.6 us (2%)
  starting transfers between devices  19.1 us (1%)
    all_to_all x1, blocking collectives, local(): lax.all_to_all(shaped, ('ba', 'col'), split_axis=2, concat_axis=1, tiled=...  447 us
    dot_general x20, matrix products, contract(): return jnp.einsum(form, table, operand, preferred_element_type=jnp.float32)  315 us
    ppermute x7, waiting for transfers between devices, local(): lax.ppermute(part, ('ba', 'col'), [(d, d ^ mask) for d in range(ways)])  247 us
    unnamed x36, local copies, waits for them, and re-layouts  112 us
    all_to_all x1, blocking collectives, local(): lax.all_to_all(conv_part, 'aa', split_axis=0, concat_axis=3, tiled=True)  97.2 us
    all_to_all x1, waiting for transfers between devices, local(): lax.all_to_all(local_block, 'aa', split_axis=3, concat_axis=0, tiled=True)  92.4 us
    all_to_all x1, local copies, waits for them, and re-layouts, local(): lax.all_to_all(local_block, 'aa', split_axis=3, concat_axis=0, tiled=True)  45.4 us
    reshape x1, local copies, waits for them, and re-layouts, local(): local_block = mixed.reshape(rows_i, rows_j, rows_k, D)  44.2 us
  transfers between devices with their start and end apart: 8, of which 5 were waited for; matrix products, arithmetic and copies ran while one was open for 2% of the time, Pallas kernels for 0%

profile of v1, /device:TPU:0, one launch (start us, length us, event | category | flops | bytes accessed | tf_op | source)
XLA Modules:
  0.0 1629.3 jit_solution(16419323245428261782)
XLA Ops:
  0.0 5.2 multiply_reduce_fusion
  5.4 5.4 fusion.14
  10.8 31.4 %fusion.236 = f32[4096,3072]{1,0:T(8,128)} fusion(bf16[4096,1024]{1,0:T(8,128)(2,1)S(1)} %fusion.14, bf16[1024,3072]{1,0:T(8,128)(2,1)S(1)} %copy-done.12), kind=kOutput, calls=%fused_computation.296 | convolution fusion | flops 25769803776 | bytes 65011712 | tf_op jit(solution)/shard_map/dot_general | solution.py:48
  42.2 15.1 fusion.4
  57.4 44.2 %copy.72 = bf16[16,8,32,1024]{2,1,0,3:T(8,128)(2,1)} copy(bf16[16,8,32,1024]{3,2,1,0:T(8,128)(2,1)} %bitcast.240) | data formatting | bytes 16777216 | tf_op jit(solution)/shard_map/reshape | solution.py:51
  101.6 50.4 %reshape.446 = bf16[4,2,524288]{2,1,0:T(2,128)(2,1)} reshape(bf16[1024,16,8,32]{3,2,1,0:T(8,128)(2,1)} %bitcast.232) | data formatting | bytes 16777216
  152.0 6.1 all-to-all-start
  159.5 92.4 %all-to-all-done = bf16[4,2,524288]{2,1,0:T(2,128)(2,1)} async-done(((bf16[4,2,524288]{2,1,0:T(2,128)(2,1)}), bf16[4,2,524288]{2,1,0:T(2,128)(2,1)}, u32[]{:S(2)}, u32[]{:S(2)}) %all-to-all-start) | async-done | bytes 8388640 | tf_op jit(solution)/shard_map/all_to_all | solution.py:52
  251.9 37.1 %reshape.447 = bf16[1024,16,8,32]{3,2,1,0:T(8,128)(2,1)} reshape(bf16[4,2,524288]{2,1,0:T(2,128)(2,1)} %all-to-all-done) | data formatting | bytes 16777216
  289.0 45.4 %copy.73 = bf16[16,8,32,4,256]{4,0,3,2,1:T(8,128)(2,1)} copy(bf16[16,8,32,4,256]{2,1,0,4,3:T(8,128)(2,1)} %bitcast.231) | data formatting | bytes 16777216 | tf_op jit(solution)/shard_map/all_to_all | solution.py:52
  334.3 6.0 fusion.107
  340.4 11.3 fusion.16
  351.7 11.4 copy_dynamic-update-slice_fusion.1
  363.1 11.5 copy_dynamic-update-slice_fusion
  374.6 8.4 broadcast_in_dim.2
  382.9 3.1 copy-done.5
  386.0 5.6 constant_dynamic-slice_fusion
  391.6 2.4 collective-permute-start
  394.1 1.5 collective-permute-start.1
  395.6 3.0 collective-permute-start.3
  399.9 39.5 %collective-permute-done = bf16[2,1,1,8,8,32,256]{6,5,4,3,2,1,0:T(8,128)(2,1)S(1)} collective-permute-done((bf16[2,1,1,8,8,32,256]{6,5,4,3,2,1,0:T(8,128)(2,1)S(1)}, bf16[2,1,1,8,8,32,256]{6,5,4,3,2,1,0:T(8,128)(2,1)S(1)}, u32[]{:S(2)}, u32[]{:S(2)}) %collective-permute-start) | collective-permute-done | bytes 2097184 | tf_op jit(solution)/shard_map/ppermute | solution.py:78
  440.8 3.8 collective-permute-start.5
  444.5 87.2 %collective-permute-done.1 = bf16[2,1,1,8,8,32,256]{6,5,4,3,2,1,0:T(8,128)(2,1)} collective-permute-done((bf16[2,1,1,8,8,32,256]{6,5,4,3,2,1,0:T(8,128)(2,1)}, bf16[2,1,1,8,8,32,256]{6,5,4,3,2,1,0:T(8,128)(2,1)}, u32[]{:S(2)}, u32[]{:S(2)}) %collective-permute-start.1) | collective-permute-done | bytes 2097184 | tf_op jit(solution)/shard_map/ppermute | solution.py:78
  535.5 1.4 copy.90
  536.8 1.4 copy.93
  538.2 3.2 constant_dynamic-update-slice_fusion.6
  541.4 3.1 constant_dynamic-update-slice_fusion.5
  544.5 29.6 %collective-permute-done.2 = bf16[2,1,1,8,8,32,256]{6,5,4,3,2,1,0:T(8,128)(2,1)} collective-permute-done((bf16[2,1,1,8,8,32,256]{6,5,4,3,2,1,0:T(8,128)(2,1)}, bf16[2,1,1,8,8,32,256]{6,5,4,3,2,1,0:T(8,128)(2,1)}, u32[]{:S(2)}, u32[]{:S(2)}) %collective-permute-start.2) | collective-permute-done | bytes 2097184 | tf_op jit(solution)/shard_map/ppermute | solution.py:78
  574.0 3.1 constant_dynamic-update-slice_fusion.4
  577.2 3.2 constant_dynamic-update-slice_fusion.3
  580.3 91.1 %collective-permute-done.4 = bf16[2,1,1,8,8,32,256]{6,5,4,3,2,1,0:T(8,128)(2,1)} collective-permute-done((bf16[2,1,1,8,8,32,256]{6,5,4,3,2,1,0:T(8,128)(2,1)}, bf16[2,1,1,8,8,32,256]{6,5,4,3,2,1,0:T(8,128)(2,1)}, u32[]{:S(2)}, u32[]{:S(2)}) %collective-permute-start.4) | collective-permute-done | bytes 2097184 | tf_op jit(solution)/shard_map/ppermute | solution.py:78
  671.4 3.1 constant_dynamic-update-slice_fusion.2
  674.6 3.1 constant_dynamic-update-slice_fusion.1
  677.7 3.1 constant_dynamic-update-slice_fusion
  680.8 10.0 fusion.227
  690.8 17.5 %fusion.45 = f32[2,8,32,256,32,1]{3,4,5,2,1,0:T(8,128)} fusion(bf16[4,2,8,8,32,256]{5,4,3,2,1,0:T(8,128)(2,1)} %bitcast.237, s32[4,8]{1,0:T(4,128)S(1)} %multiply_add_fusion), kind=kOutput, calls=%fused_computation.78 | convolution fusion | flops 268451840 | bytes 25165952 | tf_op jit(solution)/shard_map/gbj,bcfjkx->fgckx/dot_general | solution.py:31
  708.2 14.3 fusion.47
  722.6 9.0 fusion.41
  731.6 26.7 %fusion.10 = (bf16[8,32,2,32,256]{4,1,3,0,2:T(8,128)(2,1)}, bf16[8,32,2,32,256]{4,1,3,0,2:T(8,128)(2,1)}) fusion(f32[32,2,32]{0,2,1:T(8,128)S(1)} %get-tuple-element.32, f32[32,2,32]{0,2,1:T(8,128)S(1)} %get-tuple-element.31, f32[2,8,32,256,32,1]{3,4,5,2,1,0:T(8,128)} %fusion.47, f32[2,8,32,256,32,1]{3,4,5,2,1,0:T(8,128)} %fusion.45, ...), kind=kOutput, calls=%fused_computation.25 | convolution fusion | flops 310394880 | bytes 75513984 | tf_op jit(solution)/shard_map/gbj,bcfjkx->fgckx/dot_general | solution.py:31
  758.3 16.0 fusion.35
  774.3 12.4 fusion.39
  786.6 21.3 %bitcast_subtract_fusion = f32[8,32,256,64]{2,3,1,0:T(8,128)} fusion(f32[8,32,256,64,1]{2,3,4,1,0:T(8,128)} %fusion.35, bf16[8,32,2,32,256]{4,1,3,0,2:T(8,128)(2,1)} %get-tuple-element.5, s32[2,32]{1,0:T(2,128)S(1)} %multiply_add_fusion.1), kind=kOutput, calls=%fused_computation.20 | convolution fusion | flops 541130752 | bytes 41943296 | tf_op jit(solution)/shard_map/hck,fgckx->fghx/dot_general | solution.py:31
  807.9 24.5 %fusion.20 = (bf16[8,32,64,256,1]{3,2,4,1,0:T(8,128)(2,1)}, bf16[8,32,64,256,1]{3,2,4,1,0:T(8,128)(2,1)S(1)}) fusion(f32[8,32,256,64]{2,3,1,0:T(8,128)} %bitcast_subtract_fusion, bf16[2,8,32,64,256]{4,3,2,1,0:T(8,128)(2,1)} %param.10, s32[2,32]{1,0:T(2,128)S(1)} %multiply_add_fusion.1, bf16[8,32,2,32,256]{4,1,3,0,2:T(8,128)(2,1)} %get-tuple-element.6, ...), kind=kOutput, calls=%fused_computation.51 | convolution fusion | flops 583073792 | bytes 75497728 | tf_op jit(solution)/shard_map/hck,fgckx->fghx/dot_general | solution.py:31
  832.4 11.7 fusion.96
  844.1 8.2 fusion.98
  852.4 14.1 convolution_add_fusion.1
  866.5 19.4 %fusion.17 = (bf16[8,32,2,32,256,1]{4,3,2,1,0,5:T(8,128)(2,1)S(1)}, bf16[8,32,2,32,256,1]{4,3,2,1,0,5:T(8,128)(2,1)}) fusion(f32[8,32,256,2,32]{2,4,3,1,0:T(8,128)} %convolution_add_fusion.1, f32[32,2,32]{2,1,0:T(2,128)S(1)} %copy-done.10, f32[32,2,32]{2,1,0:T(2,128)S(1)} %copy-done.9, f32[8,32,256,2,32]{2,4,3,1,0:T(8,128)} %fusion.98, ...), kind=kOutput, calls=%fused_computation.48 | convolution fusion | flops 574685184 | bytes 58736896 | tf_op jit(solution)/shard_map/hck,fghx->fgckx/dot_general | solution.py:31
  885.9 11.1 fusion.33
  896.9 14.3 fusion.29
  911.3 20.0 %convolution_subtract_fusion = f32[8,2,32,256,4,8]{3,5,4,2,1,0:T(8,128)} fusion(f32[8,2,32,256,4,8]{3,5,4,2,1,0:T(8,128)} %fusion.33, bf16[8,32,2,32,256,1]{4,3,2,1,0,5:T(8,128)(2,1)} %get-tuple-element.14, s32[4,8]{1,0:T(4,128)S(1)} %multiply_add_fusion), kind=kOutput, calls=%fused_computation.43 | convolution fusion | flops 272646144 | bytes 41943168 | tf_op jit(solution)/shard_map/gbj,fgckx->bcfjkx/dot_general | solution.py:31
  931.3 23.1 %fusion.6 = (bf16[4,2,8,8,32,256]{5,3,0,4,1,2:T(8,128)(2,1)}, bf16[4,2,8,8,32,256]{5,3,0,4,1,2:T(8,128)(2,1)}) fusion(f32[8,2,32,256,4,8]{3,5,4,2,1,0:T(8,128)} %convolution_subtract_fusion, f32[4,2,8,8,32]{3,0,4,1,2:T(4,128)S(1)} %copy-done.7, f32[4,2,8,8,32]{3,0,4,1,2:T(4,128)S(1)} %copy-done.6, f32[8,2,32,256,4,8]{3,5,4,2,1,0:T(8,128)} %fusion.29, ...), kind=kOutput, calls=%fused_computation.15 | convolution fusion | flops 306200576 | bytes 58851456 | tf_op jit(solution)/shard_map/gbj,fgckx->bcfjkx/dot_general | solution.py:31
  954.4 15.8 copy.94
  970.2 15.9 copy.95
  986.1 8.0 pad_maximum_fusion
  994.1 6.8 copy.96
  1000.9 447.0 %all_to_all.36 = bf16[2,1,8,8,8,32,256]{6,5,4,3,1,0,2:T(8,128)(2,1)S(1)} all-to-all(bf16[2,1,8,8,8,32,256]{6,5,4,3,1,0,2:T(8,128)(2,1)} %copy.96), channel_id=1, replica_groups=mesh['aa'=4,'ba'=4,'col'=2] {'ba','col'}, dimensions={2} | all-to-all | bytes 33554432 | tf_op jit(solution)/shard_map/all_to_all | solution.py:137
  1447.8 5.0 fusion.226
  1452.8 12.5 fusion.23
  1465.3 21.2 %subtract_convert_fusion = bf16[64,8,32,256]{3,0,2,1:T(8,128)(2,1)} fusion(f32[64,8,32,256]{3,0,2,1:T(8,128)} %fusion.23, bf16[1,1,8,8,8,32,256]{6,5,4,3,1,0,2:T(8,128)(2,1)} %get-tuple-element.15), kind=kOutput, calls=%fused_computation.36 | convolution fusion | flops 545325056 | bytes 33554432 | tf_op jit(solution)/shard_map/fi,fjkx->ijkx/dot_general | solution.py:31
  1486.5 11.4 copy.99
  1497.9 97.2 %all_to_all.37 = bf16[64,8,32,256]{3,2,1,0:T(8,128)(2,1)S(1)} all-to-all(bf16[64,8,32,256]{3,2,1,0:T(8,128)(2,1)} %copy.99), channel_id=1, replica_groups=mesh['aa'=4,'ba'=4,'col'=2] {'aa'}, dimensions={0} | all-to-all | bytes 16777216 | tf_op jit(solution)/shard_map/all_to_all | solution.py:143
  1595.1 6.9 copy.100
  1602.0 8.2 copy.135
  1610.2 18.7 %fusion.28 = bf16[4096,1024]{1,0:T(8,128)(2,1)} fusion(bf16[1024,1024]{1,0:T(8,128)(2,1)S(1)} %copy-done, f32[4096,1024]{1,0:T(8,128)} %bitcast.246, bf16[4096,1024]{1,0:T(8,128)(2,1)S(1)} %bitcast.242, f32[4096,3072]{1,0:T(8,128)} %fusion.236, f32[1024]{0:T(1024)S(1)} %copy-done.13), kind=kOutput, calls=%fused_computation.61 | convolution fusion | flops 8619294720 | bytes 44044288 | tf_op jit(solution)/shard_map/dot_general | solution.py:148
  (53 shorter events, 8.0 us)
Async XLA Ops:
  0.0 1610.1 %copy-start = (bf16[1024,1024]{1,0:T(8,128)(2,1)S(1)}, bf16[1024,1024]{1,0:T(8,128)(2,1)}, u32[]{:S(2)}) copy-start(bf16[1024,1024]{1,0:T(8,128)(2,1)} %param.11) | copy-start | bytes 6291460
  0.0 5.4 copy-start.11
  5.4 5.4 copy-start.12
  152.0 99.9 %all-to-all-start = ((bf16[4,2,524288]{2,1,0:T(2,128)(2,1)}), bf16[4,2,524288]{2,1,0:T(2,128)(2,1)}, u32[]{:S(2)}, u32[]{:S(2)}) async-start(bf16[4,2,524288]{2,1,0:T(2,128)(2,1)} %reshape.446), calls=%async_computation | async-start | bytes 16777216 | tf_op jit(solution)/shard_map/all_to_all | solution.py:52
  334.3 6.0 copy-start.3
  374.6 11.5 copy-start.5
  391.6 47.8 %collective-permute-start = (bf16[2,1,1,8,8,32,256]{6,5,4,3,2,1,0:T(8,128)(2,1)S(1)}, bf16[2,1,1,8,8,32,256]{6,5,4,3,2,1,0:T(8,128)(2,1)S(1)}, u32[]{:S(2)}, u32[]{:S(2)}) collective-permute-start(bf16[2,1,1,8,8,32,256]{6,5,4,3,2,1,0:T(8,128)(2,1)S(1)} %get-tuple-element.25), channel_id=1, source_target_pairs={{0,1},{1,0},{2,3},{3,2},{4,5},{5,4},{6,7},{7,6},{8,9},{9,8},{10,11... | collective-permute-start | bytes 6291464 | tf_op jit(solution)/shard_map/ppermute | solution.py:78
  394.1 137.6 %collective-permute-start.1 = (bf16[2,1,1,8,8,32,256]{6,5,4,3,2,1,0:T(8,128)(2,1)}, bf16[2,1,1,8,8,32,256]{6,5,4,3,2,1,0:T(8,128)(2,1)}, u32[]{:S(2)}, u32[]{:S(2)}) collective-permute-start(bf16[2,1,1,8,8,32,256]{6,5,4,3,2,1,0:T(8,128)(2,1)} %get-tuple-element.24), channel_id=1, source_target_pairs={{0,2},{1,3},{2,0},{3,1},{4,6},{5,7},{6,4},{7,5},{8,10},{9,11},{10,... | collective-permute-start | bytes 6291464 | tf_op jit(solution)/shard_map/ppermute | solution.py:78
  395.6 178.4 %collective-permute-start.2 = (bf16[2,1,1,8,8,32,256]{6,5,4,3,2,1,0:T(8,128)(2,1)}, bf16[2,1,1,8,8,32,256]{6,5,4,3,2,1,0:T(8,128)(2,1)}, u32[]{:S(2)}, u32[]{:S(2)}) collective-permute-start(bf16[2,1,1,8,8,32,256]{6,5,4,3,2,1,0:T(8,128)(2,1)} %get-tuple-element.23), channel_id=1, source_target_pairs={{0,3},{1,2},{2,1},{3,0},{4,7},{5,6},{6,5},{7,4},{8,11},{9,10},{10,... | collective-permute-start | bytes 6291464 | tf_op jit(solution)/shard_map/ppermute | solution.py:78
  395.6 181.5 %collective-permute-start.3 = (bf16[2,1,1,8,8,32,256]{6,5,4,3,2,1,0:T(8,128)(2,1)}, bf16[2,1,1,8,8,32,256]{6,5,4,3,2,1,0:T(8,128)(2,1)}, u32[]{:S(2)}, u32[]{:S(2)}) collective-permute-start(bf16[2,1,1,8,8,32,256]{6,5,4,3,2,1,0:T(8,128)(2,1)} %get-tuple-element.22), channel_id=1, source_target_pairs={{0,4},{1,5},{2,6},{3,7},{4,0},{5,1},{6,2},{7,3},{8,12},{9,13},{10,... | collective-permute-start | bytes 6291464 | tf_op jit(solution)/shard_map/ppermute | solution.py:78
  398.6 272.8 %collective-permute-start.4 = (bf16[2,1,1,8,8,32,256]{6,5,4,3,2,1,0:T(8,128)(2,1)}, bf16[2,1,1,8,8,32,256]{6,5,4,3,2,1,0:T(8,128)(2,1)}, u32[]{:S(2)}, u32[]{:S(2)}) collective-permute-start(bf16[2,1,1,8,8,32,256]{6,5,4,3,2,1,0:T(8,128)(2,1)} %get-tuple-element.21), channel_id=1, source_target_pairs={{0,5},{1,4},{2,7},{3,6},{4,1},{5,0},{6,3},{7,2},{8,13},{9,12},{10,... | collective-permute-start | bytes 6291464 | tf_op jit(solution)/shard_map/ppermute | solution.py:78
  439.4 1.4 copy-start.8
  440.8 233.8 %collective-permute-start.5 = (bf16[2,1,1,8,8,32,256]{6,5,4,3,2,1,0:T(8,128)(2,1)}, bf16[2,1,1,8,8,32,256]{6,5,4,3,2,1,0:T(8,128)(2,1)}, u32[]{:S(2)}, u32[]{:S(2)}) collective-permute-start(bf16[2,1,1,8,8,32,256]{6,5,4,3,2,1,0:T(8,128)(2,1)} %get-tuple-element.20), channel_id=1, source_target_pairs={{0,6},{1,7},{2,4},{3,5},{4,2},{5,3},{6,0},{7,1},{8,14},{9,15},{10,... | collective-permute-start | bytes 6291464 | tf_op jit(solution)/shard_map/ppermute | solution.py:78
  531.7 145.9 %collective-permute-start.6 = (bf16[2,1,1,8,8,32,256]{6,5,4,3,2,1,0:T(8,128)(2,1)}, bf16[2,1,1,8,8,32,256]{6,5,4,3,2,1,0:T(8,128)(2,1)}, u32[]{:S(2)}, u32[]{:S(2)}) collective-permute-start(bf16[2,1,1,8,8,32,256]{6,5,4,3,2,1,0:T(8,128)(2,1)} %get-tuple-element.19), channel_id=1, source_target_pairs={{0,7},{1,6},{2,5},{3,4},{4,3},{5,2},{6,1},{7,0},{8,15},{9,14},{10,... | collective-permute-start | bytes 6291464 | tf_op jit(solution)/shard_map/ppermute | solution.py:78
  690.8 31.8 %copy-start.4 = (bf16[1,1,8,8,8,32,256]{6,5,4,3,2,1,0:T(8,128)(2,1)}, bf16[1,1,8,8,8,32,256]{6,5,4,3,2,1,0:T(8,128)(2,1)S(1)}, u32[]{:S(2)}) copy-start(bf16[1,1,8,8,8,32,256]{6,5,4,3,2,1,0:T(8,128)(2,1)S(1)} %get-tuple-element.18) | copy-start | bytes 25165828
  758.3 16.0 copy-start.1
  852.4 14.1 copy-start.9
  852.4 14.1 copy-start.10
  885.9 11.1 copy-start.2
  911.3 20.0 %copy-start.6 = (f32[4,2,8,8,32]{3,0,4,1,2:T(4,128)S(1)}, f32[4,2,8,8,32]{3,0,4,1,2:T(4,128)}, u32[]{:S(2)}) copy-start(f32[4,2,8,8,32]{3,0,4,1,2:T(4,128)} %copy.90) | copy-start | bytes 196612
  911.3 20.0 %copy-start.7 = (f32[4,2,8,8,32]{3,0,4,1,2:T(4,128)S(1)}, f32[4,2,8,8,32]{3,0,4,1,2:T(4,128)}, u32[]{:S(2)}) copy-start(f32[4,2,8,8,32]{3,0,4,1,2:T(4,128)} %copy.93) | copy-start | bytes 196612
  1595.1 15.1 slice-start
  1601.9 8.2 slice-start.1
  1602.0 8.2 copy-start.13
